TPU v7x, 256 devices: a whole 4x4x8 slice. The times are simulated.
256 devices in a mesh: grp: 8 (over x, core), lx: 4 (over y), ly: 8 (over z).
Axes of the slice: x: 4, y: 4, z: 8, core: 2. Of those that a mesh axis runs over, the one named last changes fastest.
Arguments:
- vectors: float32 [32, 256, 4096], P('grp', 'lx', 'ly'), may hold values from -6 to 6
- levels: int32 [256, 4096], P('lx', 'ly'), may hold values from 0 to 7
- level_table: float32 [8], replicated, may hold values from 1 to 3
- filter_low: float32 [1], replicated, may hold values from -1 to 0.5
- filter_high: float32 [1], replicated, may hold values from 6 to 7.5
Outputs:
- basis: float32 [32, 256, 4096], P('grp', 'lx', 'ly')
All inputs are finite; a program needn't handle non-finite values.
Results may differ from a plain program's by a relative error of at most 0.00011.
Values sent between devices are 32-bit elements; how exact they have to be, the bound alone decides.
No kernel may reach another device: no remote copies, remote signals or barrier semaphores. Data moves between devices by JAX's collectives and lax.ppermute only.
A program may use at most 64 MiB of HBM per device.

v0:
```python
import jax
import jax.numpy as jnp
from jax import lax
from jax.sharding import PartitionSpec as P


def padded_2(shard, sides, width):
    for axis, dim in sides:
        size, length = (lax.axis_size(axis), shard.shape[dim])
        up = [(i, (i + 1) % size) for i in range(size)]
        down = [(j, i) for i, j in up]
        last = lax.slice_in_dim(shard, length - width, length, axis=dim)
        leading = lax.slice_in_dim(shard, 0, width, axis=dim)
        before = lax.ppermute(last, axis, up)
        after = lax.ppermute(leading, axis, down)
        shard = jnp.concatenate([before, shard, after], axis=dim)
    return shard


def from_root(value, axis, source):
    kept = jnp.where(lax.axis_index(axis) == source, value, 0).astype(value.dtype)
    return lax.psum(kept, axis)


def apply_operator(field, onsite):
    padded = padded_2(field, (("lx", 1), ("ly", 2)), 1)
    beside = padded[:, 2:, 1:-1] + padded[:, :-2, 1:-1] + padded[:, 1:-1, 2:] + padded[:, 1:-1, :-2]
    return onsite[None] * field - beside


def lower_inverse(gram):
    lower = jnp.linalg.cholesky(gram)
    eye_block = jnp.eye(gram.shape[0], dtype=jnp.float32)
    return lax.linalg.triangular_solve(lower, eye_block, left_side=True, lower=True)


def body(vectors, levels, level_table, filter_low, filter_high):
    count_vec, rows_local, cols_local = vectors.shape
    level_ids = jnp.arange(level_table.shape[0], dtype=jnp.int32)
    onsite = jnp.sum(
        jnp.where(levels[None] == level_ids[:, None, None], level_table[:, None, None], 0.0), axis=0
    )
    center = (filter_high[0] + filter_low[0]) / 2.0
    half = (filter_high[0] - filter_low[0]) / 2.0
    first = (apply_operator(vectors, onsite) - center * vectors) / half
    filtered = 2.0 * (apply_operator(first, onsite) - center * first) / half - vectors
    total = rows_local * cols_local * lax.axis_size("lx") * lax.axis_size("ly")
    flat = filtered.reshape(count_vec, rows_local * cols_local)
    highest = lax.Precision.HIGHEST
    mine = lax.axis_index("grp")
    result = jnp.zeros_like(flat)
    for h in range(lax.axis_size("grp")):
        gram = lax.psum(jnp.dot(flat, flat.T, precision=highest), ("lx", "ly")) / total
        done = jnp.dot(lower_inverse(gram), flat, precision=highest)
        result = jnp.where(mine == h, done, result)
        shared = from_root(done, "grp", h)
        coeff = lax.psum(jnp.dot(shared, flat.T, precision=highest), ("lx", "ly")) / total
        later = mine > h
        flat = jnp.where(later, flat - jnp.dot(coeff.T, shared, precision=highest), flat)
    return result.reshape(count_vec, rows_local, cols_local)


def solution(mesh):
    in_specs = (P("grp", "lx", "ly"), P("lx", "ly"), P(), P(), P())
    out_specs = P("grp", "lx", "ly")
    return jax.shard_map(body, mesh=mesh, in_specs=in_specs, out_specs=out_specs, check_vma=False)
```

profile of v0, /device:TPU:32, one launch (start us, length us, event | category | flops | bytes accessed | tf_op | source)
XLA Modules:
  0.0 1632.8 jit_solution(7607256732290742390)
XLA Ops:
  11.9 3.5 collective-permute-done.1
  21.7 3.9 collective-permute-done.3
  31.3 3.3 collective-permute-start.6
  42.6 71.0 %psum.154 = f32[4,4]{0,1:T(4,128)S(1)} all-reduce(f32[4,4]{0,1:T(4,128)S(1)} %convolution_bitcast_fusion), channel_id=1, replica_groups=mesh['grp'=8,'lx'=4,'ly'=8] {'lx','ly'}, use_global_device_ids=true, to_apply=%region_1.2 | all-reduce | flops 16 | bytes 128 | tf_op jit(solution)/shard_map/psum | solution.py:53
  118.3 60.3 %all-reduce.8.cloned.1.call-done = f32[4,32768]{1,0:T(4,128)} async-done(((f32[4,32768]{1,0:T(4,128)}), f32[4,32768]{1,0:T(4,128)}) %all-reduce.8.cloned.1.call-update) | async-done | bytes 524304 | tf_op jit(solution)/shard_map/psum | solution.py:22
  178.6 3.5 fusion.99
  182.1 71.6 %psum.156 = f32[4,4]{0,1:T(4,128)S(1)} all-reduce(f32[4,4]{0,1:T(4,128)S(1)} %fusion.99), channel_id=1, replica_groups=mesh['grp'=8,'lx'=4,'ly'=8] {'lx','ly'}, use_global_device_ids=true, to_apply=%region_5.8 | all-reduce | flops 16 | bytes 128 | tf_op jit(solution)/shard_map/psum | solution.py:57
  257.1 73.6 %psum.157 = f32[4,4]{0,1:T(4,128)S(1)} all-reduce(f32[4,4]{0,1:T(4,128)S(1)} %fusion.100), channel_id=1, replica_groups=mesh['grp'=8,'lx'=4,'ly'=8] {'lx','ly'}, use_global_device_ids=true, to_apply=%region_6.9 | all-reduce | flops 16 | bytes 128 | tf_op jit(solution)/shard_map/psum | solution.py:53
  335.0 58.1 %all-reduce.10.cloned.1.call-done = f32[4,32768]{1,0:T(4,128)} async-done(((f32[4,32768]{1,0:T(4,128)}), f32[4,32768]{1,0:T(4,128)}) %all-reduce.10.cloned.1.call-update) | async-done | bytes 524304 | tf_op jit(solution)/shard_map/psum | solution.py:22
  393.1 3.5 fusion.101
  396.6 71.6 %psum.159 = f32[4,4]{0,1:T(4,128)S(1)} all-reduce(f32[4,4]{0,1:T(4,128)S(1)} %fusion.101), channel_id=1, replica_groups=mesh['grp'=8,'lx'=4,'ly'=8] {'lx','ly'}, use_global_device_ids=true, to_apply=%region_8.11 | all-reduce | flops 16 | bytes 128 | tf_op jit(solution)/shard_map/psum | solution.py:57
  471.6 73.6 %psum.160 = f32[4,4]{0,1:T(4,128)S(1)} all-reduce(f32[4,4]{0,1:T(4,128)S(1)} %fusion.102), channel_id=1, replica_groups=mesh['grp'=8,'lx'=4,'ly'=8] {'lx','ly'}, use_global_device_ids=true, to_apply=%region_9.12 | all-reduce | flops 16 | bytes 128 | tf_op jit(solution)/shard_map/psum | solution.py:53
  549.8 57.8 %all-reduce.12.cloned.1.call-done = f32[4,32768]{1,0:T(4,128)} async-done(((f32[4,32768]{1,0:T(4,128)}), f32[4,32768]{1,0:T(4,128)}) %all-reduce.12.cloned.1.call-update) | async-done | bytes 524304 | tf_op jit(solution)/shard_map/psum | solution.py:22
  607.6 3.5 fusion.103
  611.1 71.6 %psum.162 = f32[4,4]{0,1:T(4,128)S(1)} all-reduce(f32[4,4]{0,1:T(4,128)S(1)} %fusion.103), channel_id=1, replica_groups=mesh['grp'=8,'lx'=4,'ly'=8] {'lx','ly'}, use_global_device_ids=true, to_apply=%region_11.14 | all-reduce | flops 16 | bytes 128 | tf_op jit(solution)/shard_map/psum | solution.py:57
  686.1 73.6 %psum.163 = f32[4,4]{0,1:T(4,128)S(1)} all-reduce(f32[4,4]{0,1:T(4,128)S(1)} %fusion.104), channel_id=1, replica_groups=mesh['grp'=8,'lx'=4,'ly'=8] {'lx','ly'}, use_global_device_ids=true, to_apply=%region_12.15 | all-reduce | flops 16 | bytes 128 | tf_op jit(solution)/shard_map/psum | solution.py:53
  764.0 58.1 %all-reduce.14.cloned.1.call-done = f32[4,32768]{1,0:T(4,128)} async-done(((f32[4,32768]{1,0:T(4,128)}), f32[4,32768]{1,0:T(4,128)}) %all-reduce.14.cloned.1.call-update) | async-done | bytes 524304 | tf_op jit(solution)/shard_map/psum | solution.py:22
  822.1 3.5 fusion.105
  825.6 71.6 %psum.165 = f32[4,4]{0,1:T(4,128)S(1)} all-reduce(f32[4,4]{0,1:T(4,128)S(1)} %fusion.105), channel_id=1, replica_groups=mesh['grp'=8,'lx'=4,'ly'=8] {'lx','ly'}, use_global_device_ids=true, to_apply=%region_14.17 | all-reduce | flops 16 | bytes 128 | tf_op jit(solution)/shard_map/psum | solution.py:57
  900.6 73.6 %psum.166 = f32[4,4]{0,1:T(4,128)S(1)} all-reduce(f32[4,4]{0,1:T(4,128)S(1)} %fusion.106), channel_id=1, replica_groups=mesh['grp'=8,'lx'=4,'ly'=8] {'lx','ly'}, use_global_device_ids=true, to_apply=%region_15.18 | all-reduce | flops 16 | bytes 128 | tf_op jit(solution)/shard_map/psum | solution.py:53
  978.9 57.6 %all-reduce.16.cloned.1.call-done = f32[4,32768]{1,0:T(4,128)} async-done(((f32[4,32768]{1,0:T(4,128)}), f32[4,32768]{1,0:T(4,128)}) %all-reduce.16.cloned.1.call-update) | async-done | bytes 524304 | tf_op jit(solution)/shard_map/psum | solution.py:22
  1036.6 3.5 fusion.107
  1040.0 71.6 %psum.168 = f32[4,4]{0,1:T(4,128)S(1)} all-reduce(f32[4,4]{0,1:T(4,128)S(1)} %fusion.107), channel_id=1, replica_groups=mesh['grp'=8,'lx'=4,'ly'=8] {'lx','ly'}, use_global_device_ids=true, to_apply=%region_17.20 | all-reduce | flops 16 | bytes 128 | tf_op jit(solution)/shard_map/psum | solution.py:57
  1116.0 73.6 %psum.169 = f32[4,4]{0,1:T(4,128)S(1)} all-reduce(f32[4,4]{0,1:T(4,128)S(1)} %fusion.108), channel_id=1, replica_groups=mesh['grp'=8,'lx'=4,'ly'=8] {'lx','ly'}, use_global_device_ids=true, to_apply=%region_18.21 | all-reduce | flops 16 | bytes 128 | tf_op jit(solution)/shard_map/psum | solution.py:53
  1194.2 58.1 %all-reduce.18.cloned.1.call-done = f32[4,32768]{1,0:T(4,128)} async-done(((f32[4,32768]{1,0:T(4,128)}), f32[4,32768]{1,0:T(4,128)}) %all-reduce.18.cloned.1.call-update) | async-done | bytes 524304 | tf_op jit(solution)/shard_map/psum | solution.py:22
  1252.2 3.5 fusion.109
  1255.7 71.6 %psum.171 = f32[4,4]{0,1:T(4,128)S(1)} all-reduce(f32[4,4]{0,1:T(4,128)S(1)} %fusion.109), channel_id=1, replica_groups=mesh['grp'=8,'lx'=4,'ly'=8] {'lx','ly'}, use_global_device_ids=true, to_apply=%region_20.23 | all-reduce | flops 16 | bytes 128 | tf_op jit(solution)/shard_map/psum | solution.py:57
  1331.6 73.8 %psum.172 = f32[4,4]{0,1:T(4,128)S(1)} all-reduce(f32[4,4]{0,1:T(4,128)S(1)} %fusion.110), channel_id=1, replica_groups=mesh['grp'=8,'lx'=4,'ly'=8] {'lx','ly'}, use_global_device_ids=true, to_apply=%region_21.24 | all-reduce | flops 16 | bytes 128 | tf_op jit(solution)/shard_map/psum | solution.py:53
  1409.9 58.1 %all-reduce.20.cloned.1.call-done = f32[4,32768]{1,0:T(4,128)} async-done(((f32[4,32768]{1,0:T(4,128)}), f32[4,32768]{1,0:T(4,128)}) %all-reduce.20.cloned.1.call-update) | async-done | bytes 524304 | tf_op jit(solution)/shard_map/psum | solution.py:22
  1468.0 3.5 fusion.111
  1471.5 71.6 %psum.174 = f32[4,4]{0,1:T(4,128)S(1)} all-reduce(f32[4,4]{0,1:T(4,128)S(1)} %fusion.111), channel_id=1, replica_groups=mesh['grp'=8,'lx'=4,'ly'=8] {'lx','ly'}, use_global_device_ids=true, to_apply=%region_23.26 | all-reduce | flops 16 | bytes 128 | tf_op jit(solution)/shard_map/psum | solution.py:57
  1547.5 73.6 %psum.175 = f32[4,4]{0,1:T(4,128)S(1)} all-reduce(f32[4,4]{0,1:T(4,128)S(1)} %fusion.112), channel_id=1, replica_groups=mesh['grp'=8,'lx'=4,'ly'=8] {'lx','ly'}, use_global_device_ids=true, to_apply=%region_24.27 | all-reduce | flops 16 | bytes 128 | tf_op jit(solution)/shard_map/psum | solution.py:53
  (147 shorter events, 86.7 us)
Async XLA Ops:
  6.5 172.1 %all-reduce.8.cloned.1.call-start = ((), (), s32[]{:S(2)}) async-start(), calls=%async_computation | async-start | bytes 1048576 | tf_op jit(solution)/shard_map/psum | solution.py:22
  7.4 4.5 collective-permute-start
  10.5 8.1 copy-start.6
  10.5 15.1 copy-start
  10.5 4.9 collective-permute-start.1
  16.5 2.1 copy-start.7
  16.5 5.2 collective-permute-start.2
  16.7 9.0 collective-permute-start.3
  26.1 3.7 collective-permute-start.4
  26.2 4.9 collective-permute-start.5
  31.3 6.0 collective-permute-start.6
  34.6 5.1 collective-permute-start.7
  118.0 275.1 %all-reduce.10.cloned.1.call-start = ((), (), s32[]{:S(2)}) async-start(), calls=%async_computation.1 | async-start | bytes 1048576 | tf_op jit(solution)/shard_map/psum | solution.py:22
  178.6 75.1 %copy-start.5 = (f32[4,32768]{1,0:T(4,128)S(1)}, f32[4,32768]{1,0:T(4,128)}, u32[]{:S(2)}) copy-start(f32[4,32768]{1,0:T(4,128)} %all-reduce.8.cloned.1.call-done) | copy-start | bytes 1572868
  335.0 272.6 %all-reduce.12.cloned.1.call-start = ((), (), s32[]{:S(2)}) async-start(), calls=%async_computation.2 | async-start | bytes 1048576 | tf_op jit(solution)/shard_map/psum | solution.py:22
  393.1 75.1 %copy-start.2 = (f32[4,32768]{1,0:T(4,128)S(1)}, f32[4,32768]{1,0:T(4,128)}, u32[]{:S(2)}) copy-start(f32[4,32768]{1,0:T(4,128)} %all-reduce.10.cloned.1.call-done) | copy-start | bytes 1572868
  549.5 272.6 %all-reduce.14.cloned.1.call-start = ((), (), s32[]{:S(2)}) async-start(), calls=%async_computation.3 | async-start | bytes 1048576 | tf_op jit(solution)/shard_map/psum | solution.py:22
  607.6 75.1 %copy-start.3 = (f32[4,32768]{1,0:T(4,128)S(1)}, f32[4,32768]{1,0:T(4,128)}, u32[]{:S(2)}) copy-start(f32[4,32768]{1,0:T(4,128)} %all-reduce.12.cloned.1.call-done) | copy-start | bytes 1572868
  764.0 272.6 %all-reduce.16.cloned.1.call-start = ((), (), s32[]{:S(2)}) async-start(), calls=%async_computation.4 | async-start | bytes 1048576 | tf_op jit(solution)/shard_map/psum | solution.py:22
  822.1 75.1 %copy-start.4 = (f32[4,32768]{1,0:T(4,128)S(1)}, f32[4,32768]{1,0:T(4,128)}, u32[]{:S(2)}) copy-start(f32[4,32768]{1,0:T(4,128)} %all-reduce.14.cloned.1.call-done) | copy-start | bytes 1572868
  978.5 273.7 %all-reduce.18.cloned.1.call-start = ((), (), s32[]{:S(2)}) async-start(), calls=%async_computation.5 | async-start | bytes 1048576 | tf_op jit(solution)/shard_map/psum | solution.py:22
  1194.1 273.9 %all-reduce.20.cloned.1.call-start = ((), (), s32[]{:S(2)}) async-start(), calls=%async_computation.6 | async-start | bytes 1048576 | tf_op jit(solution)/shard_map/psum | solution.py:22
  1545.1 78.4 %copy-start.1 = (f32[4,32768]{1,0:T(4,128)S(1)}, f32[4,32768]{1,0:T(4,128)}, u32[]{:S(2)}) copy-start(f32[4,32768]{1,0:T(4,128)} %convolution_select_fusion.1) | copy-start | bytes 1572868
Sparse Core Ops, SparseCore 0:
  118.2 60.3 all-reduce.7
  335.1 57.9 all-reduce.9
  549.6 57.9 all-reduce.11
  764.1 57.9 all-reduce.13
  978.6 57.9 all-reduce.15
  1194.2 57.9 all-reduce.17
  1410.0 57.9 all-reduce.19
where the time goes:
time: 1640 us; the launch traced here: 1630 us
  blocking collectives  1090 us (66%)
  waiting for transfers between devices  427 us (26%)
  matrix products  69.2 us (4%)
  other arithmetic  19.4 us (1%)
    psum x8, blocking collectives, body(): lax.psum(jnp.dot(flat, flat.T, precision=highest), ('lx', 'ly')) / total  586 us
    psum x7, blocking collectives, body(): lax.psum(jnp.dot(shared, flat.T, precision=highest), ('lx', 'ly')) / total  501 us
    psum x7, waiting for transfers between devices, from_root(): return lax.psum(kept, axis)  408 us
  transfers between devices with their start and end apart: 15, of which 15 were waited for; matrix products, arithmetic and copies ran while one was open for 0% of the time, Pallas kernels for 0%

commit v1 on v0

--- a/solution.py
+++ b/solution.py
@@ -50,7 +50,7 @@
     mine = lax.axis_index("grp")
     result = jnp.zeros_like(flat)
     for h in range(lax.axis_size("grp")):
-        gram = lax.psum(jnp.dot(flat, flat.T, precision=highest), ("lx", "ly")) / total
+        gram = lax.psum(lax.psum(jnp.dot(flat, flat.T, precision=highest), "lx"), "ly") / total
         done = jnp.dot(lower_inverse(gram), flat, precision=highest)
         result = jnp.where(mine == h, done, result)
         shared = from_root(done, "grp", h)

time: 1640 us -> 1270 us (0.77)
  blocking collectives: 1090 us -> 706 us
    psum x8 -> x16, blocking collectives: 586 us -> 205 us  [the longest x8 142 us: body(): lax.psum(lax.psum(jnp.dot(flat, flat.T, precision=highest), 'lx'), 'ly')]
where the time goes in v1:
time: 1270 us; the launch traced here: 1260 us
  blocking collectives  706 us (56%)
  waiting for transfers between devices  437 us (34%)
  matrix products  69.2 us (5%)
  other arithmetic  19.4 us (2%)
  between operations  15.3 us (1%)
    psum x7, blocking collectives, body(): lax.psum(jnp.dot(shared, flat.T, precision=highest), ('lx', 'ly')) / total  501 us
    psum x7, waiting for transfers between devices, from_root(): return lax.psum(kept, axis)  419 us
    psum x8, blocking collectives, body(): lax.psum(lax.psum(jnp.dot(flat, flat.T, precision=highest), 'lx'), 'ly')  142 us
    psum x8, blocking collectives, body(): lax.psum(jnp.dot(flat, flat.T, precision=highest), 'lx')  62.5 us
  transfers between devices with their start and end apart: 15, of which 15 were waited for; matrix products, arithmetic and copies ran while one was open for 0% of the time, Pallas kernels for 0%

profile of v1, /device:TPU:32, one launch (start us, length us, event | category | flops | bytes accessed | tf_op | source)
XLA Modules:
  0.0 1262.0 jit_solution(13069980462268563744)
XLA Ops:
  21.7 3.9 collective-permute-done.3
  42.6 8.4 psum.210
  51.0 15.4 %psum.211 = f32[4,4]{0,1:T(4,128)S(1)} all-reduce(f32[4,4]{0,1:T(4,128)S(1)} %psum.210), channel_id=1, replica_groups=mesh['grp'=8,'lx'=4,'ly'=8] {'ly'}, use_global_device_ids=true, to_apply=%region_2.3 | all-reduce | flops 16 | bytes 128 | tf_op jit(solution)/shard_map/psum | solution.py:53
  71.2 62.1 %all-reduce.8.cloned.1.call-done = f32[4,32768]{1,0:T(4,128)} async-done(((f32[4,32768]{1,0:T(4,128)}), f32[4,32768]{1,0:T(4,128)}) %all-reduce.8.cloned.1.call-update) | async-done | bytes 524304 | tf_op jit(solution)/shard_map/psum | solution.py:22
  136.9 71.6 %psum.213 = f32[4,4]{0,1:T(4,128)S(1)} all-reduce(f32[4,4]{0,1:T(4,128)S(1)} %fusion.99), channel_id=1, replica_groups=mesh['grp'=8,'lx'=4,'ly'=8] {'lx','ly'}, use_global_device_ids=true, to_apply=%region_6.9 | all-reduce | flops 16 | bytes 128 | tf_op jit(solution)/shard_map/psum | solution.py:57
  211.8 7.7 psum.214
  219.5 18.1 %psum.215 = f32[4,4]{0,1:T(4,128)S(1)} all-reduce(f32[4,4]{0,1:T(4,128)S(1)} %psum.214), channel_id=1, replica_groups=mesh['grp'=8,'lx'=4,'ly'=8] {'ly'}, use_global_device_ids=true, to_apply=%region_8.11 | all-reduce | flops 16 | bytes 128 | tf_op jit(solution)/shard_map/psum | solution.py:53
  242.0 59.5 %all-reduce.10.cloned.1.call-done = f32[4,32768]{1,0:T(4,128)} async-done(((f32[4,32768]{1,0:T(4,128)}), f32[4,32768]{1,0:T(4,128)}) %all-reduce.10.cloned.1.call-update) | async-done | bytes 524304 | tf_op jit(solution)/shard_map/psum | solution.py:22
  301.5 3.5 fusion.101
  305.0 71.6 %psum.217 = f32[4,4]{0,1:T(4,128)S(1)} all-reduce(f32[4,4]{0,1:T(4,128)S(1)} %fusion.101), channel_id=1, replica_groups=mesh['grp'=8,'lx'=4,'ly'=8] {'lx','ly'}, use_global_device_ids=true, to_apply=%region_10.13 | all-reduce | flops 16 | bytes 128 | tf_op jit(solution)/shard_map/psum | solution.py:57
  380.0 7.7 psum.218
  387.7 18.1 %psum.219 = f32[4,4]{0,1:T(4,128)S(1)} all-reduce(f32[4,4]{0,1:T(4,128)S(1)} %psum.218), channel_id=1, replica_groups=mesh['grp'=8,'lx'=4,'ly'=8] {'ly'}, use_global_device_ids=true, to_apply=%region_12.15 | all-reduce | flops 16 | bytes 128 | tf_op jit(solution)/shard_map/psum | solution.py:53
  410.4 59.3 %all-reduce.12.cloned.1.call-done = f32[4,32768]{1,0:T(4,128)} async-done(((f32[4,32768]{1,0:T(4,128)}), f32[4,32768]{1,0:T(4,128)}) %all-reduce.12.cloned.1.call-update) | async-done | bytes 524304 | tf_op jit(solution)/shard_map/psum | solution.py:22
  473.2 71.6 %psum.221 = f32[4,4]{0,1:T(4,128)S(1)} all-reduce(f32[4,4]{0,1:T(4,128)S(1)} %fusion.103), channel_id=1, replica_groups=mesh['grp'=8,'lx'=4,'ly'=8] {'lx','ly'}, use_global_device_ids=true, to_apply=%region_14.17 | all-reduce | flops 16 | bytes 128 | tf_op jit(solution)/shard_map/psum | solution.py:57
  548.2 7.7 psum.222
  555.9 18.1 %psum.223 = f32[4,4]{0,1:T(4,128)S(1)} all-reduce(f32[4,4]{0,1:T(4,128)S(1)} %psum.222), channel_id=1, replica_groups=mesh['grp'=8,'lx'=4,'ly'=8] {'ly'}, use_global_device_ids=true, to_apply=%region_16.19 | all-reduce | flops 16 | bytes 128 | tf_op jit(solution)/shard_map/psum | solution.py:53
  578.4 59.5 %all-reduce.14.cloned.1.call-done = f32[4,32768]{1,0:T(4,128)} async-done(((f32[4,32768]{1,0:T(4,128)}), f32[4,32768]{1,0:T(4,128)}) %all-reduce.14.cloned.1.call-update) | async-done | bytes 524304 | tf_op jit(solution)/shard_map/psum | solution.py:22
  641.4 71.6 %psum.225 = f32[4,4]{0,1:T(4,128)S(1)} all-reduce(f32[4,4]{0,1:T(4,128)S(1)} %fusion.105), channel_id=1, replica_groups=mesh['grp'=8,'lx'=4,'ly'=8] {'lx','ly'}, use_global_device_ids=true, to_apply=%region_18.21 | all-reduce | flops 16 | bytes 128 | tf_op jit(solution)/shard_map/psum | solution.py:57
  716.3 7.7 psum.226
  724.1 18.1 %psum.227 = f32[4,4]{0,1:T(4,128)S(1)} all-reduce(f32[4,4]{0,1:T(4,128)S(1)} %psum.226), channel_id=1, replica_groups=mesh['grp'=8,'lx'=4,'ly'=8] {'ly'}, use_global_device_ids=true, to_apply=%region_20.23 | all-reduce | flops 16 | bytes 128 | tf_op jit(solution)/shard_map/psum | solution.py:53
  747.0 59.1 %all-reduce.16.cloned.1.call-done = f32[4,32768]{1,0:T(4,128)} async-done(((f32[4,32768]{1,0:T(4,128)}), f32[4,32768]{1,0:T(4,128)}) %all-reduce.16.cloned.1.call-update) | async-done | bytes 524304 | tf_op jit(solution)/shard_map/psum | solution.py:22
  809.5 71.6 %psum.229 = f32[4,4]{0,1:T(4,128)S(1)} all-reduce(f32[4,4]{0,1:T(4,128)S(1)} %fusion.107), channel_id=1, replica_groups=mesh['grp'=8,'lx'=4,'ly'=8] {'lx','ly'}, use_global_device_ids=true, to_apply=%region_22.25 | all-reduce | flops 16 | bytes 128 | tf_op jit(solution)/shard_map/psum | solution.py:57
  885.5 7.7 psum.230
  893.2 18.1 %psum.231 = f32[4,4]{0,1:T(4,128)S(1)} all-reduce(f32[4,4]{0,1:T(4,128)S(1)} %psum.230), channel_id=1, replica_groups=mesh['grp'=8,'lx'=4,'ly'=8] {'ly'}, use_global_device_ids=true, to_apply=%region_24.27 | all-reduce | flops 16 | bytes 128 | tf_op jit(solution)/shard_map/psum | solution.py:53
  915.9 59.5 %all-reduce.18.cloned.1.call-done = f32[4,32768]{1,0:T(4,128)} async-done(((f32[4,32768]{1,0:T(4,128)}), f32[4,32768]{1,0:T(4,128)}) %all-reduce.18.cloned.1.call-update) | async-done | bytes 524304 | tf_op jit(solution)/shard_map/psum | solution.py:22
  978.8 71.6 %psum.233 = f32[4,4]{0,1:T(4,128)S(1)} all-reduce(f32[4,4]{0,1:T(4,128)S(1)} %fusion.109), channel_id=1, replica_groups=mesh['grp'=8,'lx'=4,'ly'=8] {'lx','ly'}, use_global_device_ids=true, to_apply=%region_26.29 | all-reduce | flops 16 | bytes 128 | tf_op jit(solution)/shard_map/psum | solution.py:57
  1054.8 7.7 psum.234
  1062.5 18.3 %psum.235 = f32[4,4]{0,1:T(4,128)S(1)} all-reduce(f32[4,4]{0,1:T(4,128)S(1)} %psum.234), channel_id=1, replica_groups=mesh['grp'=8,'lx'=4,'ly'=8] {'ly'}, use_global_device_ids=true, to_apply=%region_28.31 | all-reduce | flops 16 | bytes 128 | tf_op jit(solution)/shard_map/psum | solution.py:53
  1085.3 59.6 %all-reduce.20.cloned.1.call-done = f32[4,32768]{1,0:T(4,128)} async-done(((f32[4,32768]{1,0:T(4,128)}), f32[4,32768]{1,0:T(4,128)}) %all-reduce.20.cloned.1.call-update) | async-done | bytes 524304 | tf_op jit(solution)/shard_map/psum | solution.py:22
  1148.4 71.6 %psum.237 = f32[4,4]{0,1:T(4,128)S(1)} all-reduce(f32[4,4]{0,1:T(4,128)S(1)} %fusion.111), channel_id=1, replica_groups=mesh['grp'=8,'lx'=4,'ly'=8] {'lx','ly'}, use_global_device_ids=true, to_apply=%region_30.33 | all-reduce | flops 16 | bytes 128 | tf_op jit(solution)/shard_map/psum | solution.py:57
  1224.4 7.7 psum.238
  1232.1 18.1 %psum.239 = f32[4,4]{0,1:T(4,128)S(1)} all-reduce(f32[4,4]{0,1:T(4,128)S(1)} %psum.238), channel_id=1, replica_groups=mesh['grp'=8,'lx'=4,'ly'=8] {'ly'}, use_global_device_ids=true, to_apply=%region_32.35 | all-reduce | flops 16 | bytes 128 | tf_op jit(solution)/shard_map/psum | solution.py:53
  (155 shorter events, 114.5 us)
Async XLA Ops:
  6.5 126.8 %all-reduce.8.cloned.1.call-start = ((), (), s32[]{:S(2)}) async-start(), calls=%async_computation | async-start | bytes 1048576 | tf_op jit(solution)/shard_map/psum | solution.py:22
  7.4 4.5 collective-permute-start
  10.5 8.1 copy-start.6
  10.5 15.1 %copy-start = (f32[4,64,512]{2,1,0:T(8,128)S(1)}, f32[4,64,512]{2,1,0:T(8,128)}, u32[]{:S(2)}) copy-start(f32[4,64,512]{2,1,0:T(8,128)} %param.8) | copy-start | bytes 1572868
  10.5 4.9 collective-permute-start.1
  16.5 2.1 copy-start.7
  16.5 5.2 collective-permute-start.2
  16.7 9.0 collective-permute-start.3
  26.1 3.7 collective-permute-start.4
  26.2 4.9 collective-permute-start.5
  31.3 6.0 collective-permute-start.6
  34.6 5.1 collective-permute-start.7
  71.0 230.6 %all-reduce.10.cloned.1.call-start = ((), (), s32[]{:S(2)}) async-start(), calls=%async_computation.1 | async-start | bytes 1048576 | tf_op jit(solution)/shard_map/psum | solution.py:22
  133.3 75.1 %copy-start.5 = (f32[4,32768]{1,0:T(4,128)S(1)}, f32[4,32768]{1,0:T(4,128)}, u32[]{:S(2)}) copy-start(f32[4,32768]{1,0:T(4,128)} %all-reduce.8.cloned.1.call-done) | copy-start | bytes 1572868
  242.0 227.7 %all-reduce.12.cloned.1.call-start = ((), (), s32[]{:S(2)}) async-start(), calls=%async_computation.2 | async-start | bytes 1048576 | tf_op jit(solution)/shard_map/psum | solution.py:22
  301.5 75.1 %copy-start.2 = (f32[4,32768]{1,0:T(4,128)S(1)}, f32[4,32768]{1,0:T(4,128)}, u32[]{:S(2)}) copy-start(f32[4,32768]{1,0:T(4,128)} %all-reduce.10.cloned.1.call-done) | copy-start | bytes 1572868
  410.1 227.7 %all-reduce.14.cloned.1.call-start = ((), (), s32[]{:S(2)}) async-start(), calls=%async_computation.3 | async-start | bytes 1048576 | tf_op jit(solution)/shard_map/psum | solution.py:22
  469.7 75.1 %copy-start.3 = (f32[4,32768]{1,0:T(4,128)S(1)}, f32[4,32768]{1,0:T(4,128)}, u32[]{:S(2)}) copy-start(f32[4,32768]{1,0:T(4,128)} %all-reduce.12.cloned.1.call-done) | copy-start | bytes 1572868
  578.3 227.7 %all-reduce.16.cloned.1.call-start = ((), (), s32[]{:S(2)}) async-start(), calls=%async_computation.4 | async-start | bytes 1048576 | tf_op jit(solution)/shard_map/psum | solution.py:22
  637.9 75.1 %copy-start.4 = (f32[4,32768]{1,0:T(4,128)S(1)}, f32[4,32768]{1,0:T(4,128)}, u32[]{:S(2)}) copy-start(f32[4,32768]{1,0:T(4,128)} %all-reduce.14.cloned.1.call-done) | copy-start | bytes 1572868
  746.5 228.9 %all-reduce.18.cloned.1.call-start = ((), (), s32[]{:S(2)}) async-start(), calls=%async_computation.5 | async-start | bytes 1048576 | tf_op jit(solution)/shard_map/psum | solution.py:22
  915.8 229.1 %all-reduce.20.cloned.1.call-start = ((), (), s32[]{:S(2)}) async-start(), calls=%async_computation.6 | async-start | bytes 1048576 | tf_op jit(solution)/shard_map/psum | solution.py:22
  1222.0 30.6 %copy-start.1 = (f32[4,32768]{1,0:T(4,128)S(1)}, f32[4,32768]{1,0:T(4,128)}, u32[]{:S(2)}) copy-start(f32[4,32768]{1,0:T(4,128)} %convolution_select_fusion.1) | copy-start | bytes 1572868
Sparse Core Ops, SparseCore 0:
  71.1 62.2 all-reduce.7
  242.1 59.3 all-reduce.9
  410.3 59.3 all-reduce.11
  578.4 59.3 all-reduce.13
  746.6 59.3 all-reduce.15
  915.9 59.3 all-reduce.17
  1085.4 59.4 all-reduce.19
